TPU v7x, 256 devices: a whole 4x4x8 slice. The times are simulated.
256 devices in a mesh: mp: 2 (over core), dev: 128 (over y, x, z).
Axes of the slice: x: 4, y: 4, z: 8, core: 2. Of those that a mesh axis runs over, the one named last changes fastest.
Arguments:
- spectrum: float32 [1024, 65536], P(None, ('mp', 'dev')), may hold values from 0.05 to 1
- water_mask: int32 [65536], P(('mp', 'dev')), may hold values 0 or 1
- courant: float32 [2, 1024], replicated, may hold values from 0.05 to 0.3
- stencil_sign: int32 [2, 1024], replicated, may hold values from 0 to 1
- quad_index: int32 [4, 1024, 2], replicated, may hold values from 0 to 1023
- quad_weight: float32 [4, 1024, 2], replicated, may hold values from 0.2 to 1
- nonlinear: float32 [1024], replicated, may hold values from 0.01 to 0.1
- stokes_table: bfloat16 [128, 1024], replicated, may hold values from -0.1875 to 0.1875
- point_index: int32 [4, 65536], P(None, ('mp', 'dev')), may hold values from 0 to 32767, as said below
- point_weight: float32 [4, 65536], P(None, ('mp', 'dev')), may hold values from 0.1 to 0.4
- ocean_index: int32 [4, 32768], P(None, ('mp', 'dev')), may hold values from 0 to 65535, as said below
- ocean_weight: float32 [4, 32768], P(None, ('mp', 'dev')), may hold values from 0.1 to 0.4
- currents: float32 [2, 64, 32768], P(None, None, ('mp', 'dev')), may hold values from -3 to 3
- coriolis: float32 [32768], P(('mp', 'dev')), may hold values from 0.2 to 0.6
- mixing: float32 [64], replicated, may hold values from 0.05 to 0.2
- surface_weights: float32 [64], replicated, may hold values from 0.005 to 0.05
Outputs:
- spectrum_out: float32 [1024, 65536], P(None, ('mp', 'dev'))
- currents_out: float32 [2, 64, 32768], P(None, None, ('mp', 'dev'))
Inputs may be any that keep to these rules, and one draw needn't show every extreme that they name: `point_index`: entry j of point p names an ocean cell in row p // 256 plus -1, 0 or 1 and column (p % 256) // 2 plus -1, 0 or 1, both wrapping. `ocean_index`: entry j of cell c names a wave point in row c // 128 plus -1, 0 or 1 and column 2 (c % 128) plus -2 to 3, both wrapping.
All inputs are finite; a program needn't handle non-finite values. No bound on the sum of `water_mask` on one device may be relied on, other than what follows from the above.
Results may differ from a plain program's by a relative error of at most 0.0003.
The roundings to bfloat16 on the way count: a program that leaves them out, or rounds other values in their place, can miss the bound.
Values sent between devices are 32-bit elements; how exact they have to be, the bound alone decides.
No kernel may reach another device: no remote copies, remote signals or barrier semaphores. Data moves between devices by JAX's collectives and lax.ppermute only.
A program may use at most 64 MiB of HBM per device.

v0:
```python
import jax
import jax.numpy as jnp
from jax import lax
from jax.sharding import PartitionSpec as P

K = 1024
L = 64
MX = 256
ROWS_DEV = 1
STEPS = 2
OX = 128


ocean_step_size = 0.5


def padded_2(array, sides, width):
    edges = {}
    for axis, dim in sides:
        count, length = (lax.axis_size(axis), array.shape[dim])
        up = [(i, (i + 1) % count) for i in range(count)]
        last = lax.slice_in_dim(array, length - width, length, axis=dim)
        first = lax.slice_in_dim(array, 0, width, axis=dim)
        edges[dim] = (
            lax.ppermute(last, axis, up),
            lax.ppermute(first, axis, [(b, a) for a, b in up]),
        )
    done = []
    for _, dim in sides:
        low, high = edges[dim]
        around = [(width, width) if d in done else (0, 0) for d in range(array.ndim)]
        array = jnp.concatenate([jnp.pad(low, around), array, jnp.pad(high, around)], axis=dim)
        done.append(dim)
    return array


def padded_3(cells, sides, width):
    for axis, dim in sides:
        count = lax.axis_size(axis)
        head = lax.slice_in_dim(cells, 0, width, axis=dim)
        tail = lax.slice_in_dim(cells, cells.shape[dim] - width, cells.shape[dim], axis=dim)
        cells = jnp.concatenate(
            [
                lax.ppermute(tail, axis, [(i, (i + 1) % count) for i in range(count)]),
                cells,
                lax.ppermute(head, axis, [((i + 1) % count, i) for i in range(count)]),
            ],
            axis=dim,
        )
    return cells


def advect(spectra, padded, point_flow, courant, stencil_sign):
    eastward = stencil_sign[0][:, None, None] == 1
    northward = stencil_sign[1][:, None, None] == 1
    sense_x = (2 * stencil_sign[0] - 1).astype(jnp.float32)[:, None, None]
    sense_y = (2 * stencil_sign[1] - 1).astype(jnp.float32)[:, None, None]
    behind_x = jnp.where(eastward, jnp.roll(spectra, 1, axis=2), jnp.roll(spectra, -1, axis=2))
    behind_y = jnp.where(northward, padded[:, :-2], padded[:, 2:])
    speed_x = courant[0][:, None, None] * (1.0 + 0.5 * jnp.tanh(sense_x * point_flow[0][None]))
    speed_y = courant[1][:, None, None] * (1.0 + 0.5 * jnp.tanh(sense_y * point_flow[1][None]))
    return spectra - speed_x * (spectra - behind_x) - speed_y * (spectra - behind_y)


def quad_table(row_index, weight, span_width):
    columns = jnp.arange(span_width, dtype=jnp.int32)[None, :]
    first_part = jnp.where(row_index[:, 0:1] == columns, weight[:, 0:1], 0.0)
    second = jnp.where(row_index[:, 1:2] == columns, weight[:, 1:2], 0.0)
    return (first_part + second).astype(jnp.bfloat16)


def spread_table(local_index, weight, wide_count):
    slots = jnp.arange(wide_count, dtype=jnp.int32)[:, None]
    total = jnp.zeros((wide_count, local_index.shape[1]), jnp.float32)
    for config in range(4):
        total = total + jnp.where(
            local_index[config][None, :] == slots, weight[config][None, :], 0.0
        )
    return total


def nonlinear_update(advected, interps, gain_rows, wet_row):
    total_sum = interps[0] + interps[1] + interps[2] + interps[3]
    pair_sum = interps[0] * interps[1] + interps[2] * interps[3]
    source = advected * advected * total_sum - advected * pair_sum
    return wet_row[None, :] * (advected + gain_rows[:, None] * source)


def vertical_mix(profile, mixing):
    above_level = jnp.concatenate([profile[:1], profile[:-1]], axis=0)
    below_level = jnp.concatenate([profile[1:], profile[-1:]], axis=0)
    return mixing[:, None, None] * (above_level - 2.0 * profile + below_level)


def ocean_prepare(zonal_flow, meridional, mixing):
    padded_zonal = padded_2(zonal_flow, ((("mp", "dev"), 1),), 1)
    vorticity = 0.5 * (jnp.roll(meridional, -1, axis=2) - jnp.roll(meridional, 1, axis=2)) - 0.5 * (
        padded_zonal[:, 2:] - padded_zonal[:, :-2]
    )
    return (vorticity, vertical_mix(zonal_flow, mixing), vertical_mix(meridional, mixing))


def ocean_advance(zonal_flow, meridional, tendency, stokes_drift, rotation):
    vorticity, mix_zonal, mix_meridional = tendency
    drift_x = stokes_drift[0]
    drift_y = stokes_drift[1]
    new_zonal = zonal_flow + ocean_step_size * (
        rotation[None] * (meridional + drift_y) + vorticity * drift_y + mix_zonal
    )
    new_meridional = meridional + ocean_step_size * (
        -rotation[None] * (zonal_flow + drift_x) - vorticity * drift_x + mix_meridional
    )
    return jnp.stack([new_zonal, new_meridional])


def transport(spectra, point_flow, courant, stencil_sign):
    comp_total = spectra.shape[0]
    map_grid = spectra.reshape(comp_total, -1, MX)
    padded = padded_2(map_grid, ((("mp", "dev"), 1),), 1)
    shifted = advect(map_grid, padded, point_flow.reshape(2, -1, MX), courant, stencil_sign)
    return shifted.reshape(comp_total, -1)


def sources(advected, quad_tables, nonlinear, wet_points):
    rounded = advected.astype(jnp.bfloat16)
    interps = [
        jnp.dot(quad_tables[config], rounded, preferred_element_type=jnp.float32)
        for config in range(4)
    ]
    return nonlinear_update(advected, interps, nonlinear, wet_points)


def local(
    spectrum,
    water_mask,
    courant,
    stencil_sign,
    quad_index,
    quad_weight,
    nonlinear,
    stokes_table,
    point_index,
    point_weight,
    ocean_index,
    ocean_weight,
    currents,
    coriolis,
    mixing,
    surface_weights,
):
    devices = lax.axis_size("mp") * lax.axis_size("dev")
    position = lax.axis_index(("mp", "dev"))
    local_points = spectrum.shape[1]
    local_cells = currents.shape[2]
    cell_local = jnp.mod(point_index - position * local_cells + OX, local_cells * devices)
    point_local = jnp.mod(ocean_index - position * local_points + MX, local_points * devices)
    surface_spread = spread_table(cell_local, point_weight, local_cells + 2 * OX)
    stokes_spread = spread_table(point_local, ocean_weight, local_points + 2 * MX)
    quad_tables = [quad_table(quad_index[config], quad_weight[config], K) for config in range(4)]
    wet_points = water_mask.astype(jnp.float32)
    rotation = coriolis.reshape(ROWS_DEV, OX)
    ocean_state = currents
    spectra = spectrum
    for step_index in range(STEPS):
        zonal_flow = ocean_state[0].reshape(L, ROWS_DEV, OX)
        meridional = ocean_state[1].reshape(L, ROWS_DEV, OX)
        surface = jnp.sum(surface_weights[None, :, None] * ocean_state, axis=1)
        surface_wide = padded_2(surface, ((("mp", "dev"), 1),), OX)
        point_flow = jnp.dot(surface_wide, surface_spread, precision=lax.Precision.HIGHEST)
        advected = transport(spectra, point_flow, courant, stencil_sign)
        spectra = sources(advected, quad_tables, nonlinear, wet_points)
        stokes = jnp.dot(
            stokes_table, spectra.astype(jnp.bfloat16), preferred_element_type=jnp.float32
        )
        stokes_wide = padded_3(stokes, ((("mp", "dev"), 1),), MX)
        stokes_drift = jnp.dot(stokes_wide, stokes_spread, precision=lax.Precision.HIGHEST)
        stokes_drift = stokes_drift.reshape(2, L, ROWS_DEV, OX)
        tendency = ocean_prepare(zonal_flow, meridional, mixing)
        ocean_state = ocean_advance(
            zonal_flow, meridional, tendency, stokes_drift, rotation
        ).reshape(2, L, ROWS_DEV * OX)
    return (spectra, ocean_state)


def solution(mesh):
    return jax.shard_map(
        local,
        mesh=mesh,
        in_specs=(
            P(None, ("mp", "dev")),
            P(("mp", "dev")),
            P(),
            P(),
            P(),
            P(),
            P(),
            P(),
            P(None, ("mp", "dev")),
            P(None, ("mp", "dev")),
            P(None, ("mp", "dev")),
            P(None, ("mp", "dev")),
            P(None, None, ("mp", "dev")),
            P(("mp", "dev")),
            P(),
            P(),
        ),
        out_specs=(P(None, ("mp", "dev")), P(None, None, ("mp", "dev"))),
        check_vma=False,
    )
```

profile of v0, /device:TPU:1, one launch (start us, length us, event | category | flops | bytes accessed | tf_op | source)
XLA Modules:
  0.0 119.1 jit_solution(2582976475012336717)
XLA Ops:
  0.6 1.6 %multiply_reduce_fusion = f32[2,128]{1,0:T(2,128)} fusion(f32[2,64,128]{2,1,0:T(8,128)} %param.28, f32[64]{0:T(128)} %param.31), kind=kLoop, calls=%fused_computation.108 | loop fusion | flops 32512 | bytes 66816 | tf_op jit(solution)/shard_map/reduce_sum | solution.py:167
  2.2 2.5 %collective-permute-start = (f32[2,128]{1,0:T(2,128)}, f32[2,128]{1,0:T(2,128)}, u32[]{:S(2)}, u32[]{:S(2)}) collective-permute-start(f32[2,128]{1,0:T(2,128)} %multiply_reduce_fusion), channel_id=1, source_target_pairs={{0,1},{1,2},{2,3},{3,4},{4,5},{5,6},{6,7},{7,8},{8,9},{9,10},{10,1... | collective-permute-start | bytes 3080 | tf_op jit(solution)/shard_map/ppermute | solution.py:25
  4.8 9.2 %collective-permute-start.1 = (f32[2,128]{1,0:T(2,128)}, f32[2,128]{1,0:T(2,128)}, u32[]{:S(2)}, u32[]{:S(2)}) collective-permute-start(f32[2,128]{1,0:T(2,128)} %multiply_reduce_fusion), channel_id=1, source_target_pairs={{1,0},{2,1},{3,2},{4,3},{5,4},{6,5},{7,6},{8,7},{9,8},{10,9},{11,1... | collective-permute-start | bytes 3080 | tf_op jit(solution)/shard_map/ppermute | solution.py:26
  14.0 1.6 %copy.20 = f32[1024,256]{0,1:T(8,128)S(1)} copy(f32[1024,256]{1,0:T(8,128)} %param.16) | data formatting | bytes 2097152 | tf_op args[0]
  15.7 7.2 %collective-permute-start.3 = (f32[1024,1,256]{0,2,1:T(8,128)S(1)}, f32[1024,1,256]{0,2,1:T(8,128)S(1)}, u32[]{:S(2)}, u32[]{:S(2)}) collective-permute-start(f32[1024,1,256]{0,2,1:T(8,128)S(1)} %bitcast.195), channel_id=1, source_target_pairs={{1,0},{2,1},{3,2},{4,3},{5,4},{6,5},{7,6},{8,7},{9,8},{10,9},{11,1... | collective-permute-start | bytes 3145736 | tf_op jit(solution)/shard_map/ppermute | solution.py:26
  27.9 1.4 %slice_bitcast_fusion.15 = (s32[1024,2]{0,1:T(2,128)S(1)}, s32[1024,2]{0,1:T(2,128)}, s32[1024,2]{0,1:T(2,128)}, s32[1024,2]{0,1:T(2,128)}) fusion(s32[4,1024,2]{1,2,0:T(2,128)} %param.20), kind=kLoop, calls=%fused_computation.162 | loop fusion | bytes 65536 | tf_op jit(solution)/shard_map/squeeze | solution.py:159
  29.3 1.3 %slice_bitcast_fusion.14 = (f32[1024,2]{0,1:T(2,128)S(1)}, f32[1024,2]{0,1:T(2,128)S(1)}, f32[1024,2]{0,1:T(2,128)}, f32[1024,2]{0,1:T(2,128)}) fusion(f32[4,1024,2]{1,2,0:T(2,128)} %param.21), kind=kLoop, calls=%fused_computation.161 | loop fusion | bytes 65536 | tf_op jit(solution)/shard_map/squeeze | solution.py:159
  35.3 1.6 %collective-permute-start.7 = (f32[64,1,128]{2,0,1:T(8,128)}, f32[64,1,128]{2,0,1:T(8,128)S(1)}, u32[]{:S(2)}, u32[]{:S(2)}) collective-permute-start(f32[64,1,128]{2,0,1:T(8,128)} %get-tuple-element.23), channel_id=1, source_target_pairs={{0,1},{1,2},{2,3},{3,4},{4,5},{5,6},{6,7},{7,8},{8,9},{9,10},{10,1... | collective-permute-start | bytes 98312 | tf_op jit(solution)/shard_map/ppermute | solution.py:25
  38.1 7.9 %collective-permute-done.2 = f32[1024,1,256]{0,2,1:T(8,128)S(1)} collective-permute-done((f32[1024,1,256]{0,2,1:T(8,128)S(1)}, f32[1024,1,256]{0,2,1:T(8,128)S(1)}, u32[]{:S(2)}, u32[]{:S(2)}) %collective-permute-start.2) | collective-permute-done | bytes 1048608 | tf_op jit(solution)/shard_map/ppermute | solution.py:25
  47.0 2.3 %fusion.1 = f32[1024,256]{0,1:T(8,128)S(1)} fusion(bf16[1024,256]{0,1:T(8,128)(2,1)S(1)} %get-tuple-element.12, f32[1024]{0:T(1024)S(1)} %bitcast.234, s32[1024]{0:T(1024)S(1)} %bitcast.226, f32[1024]{0:T(1024)S(1)} %bitcast.232, s32[1024]{0:T(1024)S(1)} %bitcast.224), kind=kOutput, calls=%fused_computation.13 | convolution fusion | flops 543162368 | bytes 1589248 | tf_op jit(solution)/shard_map/dot_general | solution.py:127
  49.3 2.3 %fusion.3 = f32[1024,256]{0,1:T(8,128)S(1)} fusion(bf16[1024,256]{0,1:T(8,128)(2,1)S(1)} %get-tuple-element.12, f32[1024]{0:T(1024)S(1)} %bitcast.244, s32[1024]{0:T(1024)S(1)} %bitcast.240, f32[1024]{0:T(1024)S(1)} %bitcast.246, s32[1024]{0:T(1024)S(1)} %bitcast.242), kind=kOutput, calls=%fused_computation.15 | convolution fusion | flops 543162368 | bytes 1589248 | tf_op jit(solution)/shard_map/dot_general | solution.py:127
  51.6 2.3 %fusion.7 = f32[1024,256]{0,1:T(8,128)S(1)} fusion(bf16[1024,256]{0,1:T(8,128)(2,1)S(1)} %get-tuple-element.12, f32[1024]{0:T(1024)S(1)} %bitcast.220, s32[1024]{0:T(1024)S(1)} %bitcast.216, f32[1024]{0:T(1024)S(1)} %bitcast.222, s32[1024]{0:T(1024)S(1)} %bitcast.218), kind=kOutput, calls=%fused_computation.19 | convolution fusion | flops 543162368 | bytes 1589248 | tf_op jit(solution)/shard_map/dot_general | solution.py:127
  53.9 1.9 %add_multiply_fusion.1 = f32[1024,256]{0,1:T(8,128)S(1)} fusion(f32[1024,256]{0,1:T(8,128)S(1)} %get-tuple-element.13, f32[1024,256]{0,1:T(8,128)S(1)} %fusion.7, f32[1024,256]{0,1:T(8,128)S(1)} %fusion.1, f32[1024,256]{0,1:T(8,128)S(1)} %fusion.3, f32[1024]{0:T(1024)S(1)} %copy-done.39, f32[256]{0:T(256)S(1)} %convert_element_type.49, ...), kind=kOutput, calls=%fused_computation.41 | convolution fusion | flops 546570240 | bytes 5788672 | tf_op jit(solution)/shard_map/dot_general | solution.py:127
  56.2 7.9 %collective-permute-start.5 = (f32[128,256]{0,1:T(8,128)S(1)}, f32[128,256]{0,1:T(8,128)S(1)}, u32[]{:S(2)}, u32[]{:S(2)}) collective-permute-start(f32[128,256]{0,1:T(8,128)S(1)} %convolution_bitcast_fusion.1), channel_id=1, source_target_pairs={{1,0},{2,1},{3,2},{4,3},{5,4},{6,5},{7,6},{8,7},{9,8},{10,9},{11,1... | collective-permute-start | bytes 393224 | tf_op jit(solution)/shard_map/ppermute | solution.py:46
  64.6 2.9 %collective-permute-done.4 = f32[128,256]{0,1:T(8,128)S(1)} collective-permute-done((f32[128,256]{0,1:T(8,128)S(1)}, f32[128,256]{0,1:T(8,128)S(1)}, u32[]{:S(2)}, u32[]{:S(2)}) %collective-permute-start.4) | collective-permute-done | bytes 131104 | tf_op jit(solution)/shard_map/ppermute | solution.py:44
  67.5 4.3 %collective-permute-start.11 = (f32[1024,1,256]{0,2,1:T(8,128)S(1)}, f32[1024,1,256]{0,2,1:T(8,128)S(1)}, u32[]{:S(2)}, u32[]{:S(2)}) collective-permute-start(f32[1024,1,256]{0,2,1:T(8,128)S(1)} %bitcast.201), channel_id=1, source_target_pairs={{1,0},{2,1},{3,2},{4,3},{5,4},{6,5},{7,6},{8,7},{9,8},{10,9},{11,1... | collective-permute-start | bytes 3145736 | tf_op jit(solution)/shard_map/ppermute | solution.py:26
  74.1 7.2 %collective-permute-start.9 = (f32[2,128]{1,0:T(2,128)S(1)}, f32[2,128]{1,0:T(2,128)S(1)}, u32[]{:S(2)}, u32[]{:S(2)}) collective-permute-start(f32[2,128]{1,0:T(2,128)S(1)} %fusion.73), channel_id=1, source_target_pairs={{1,0},{2,1},{3,2},{4,3},{5,4},{6,5},{7,6},{8,7},{9,8},{10,9},{11,1... | collective-permute-start | bytes 3080 | tf_op jit(solution)/shard_map/ppermute | solution.py:26
  81.5 13.6 %collective-permute-done.8 = f32[2,128]{1,0:T(2,128)S(1)} collective-permute-done((f32[2,128]{1,0:T(2,128)S(1)}, f32[2,128]{1,0:T(2,128)S(1)}, u32[]{:S(2)}, u32[]{:S(2)}) %collective-permute-start.8) | collective-permute-done | bytes 1056 | tf_op jit(solution)/shard_map/ppermute | solution.py:25
  96.5 2.3 %fusion = f32[1024,256]{0,1:T(8,128)S(1)} fusion(bf16[1024,256]{0,1:T(8,128)(2,1)S(1)} %get-tuple-element.8, f32[1024]{0:T(1024)S(1)} %bitcast.235, s32[1024]{0:T(1024)S(1)} %bitcast.227, f32[1024]{0:T(1024)S(1)} %bitcast.233, s32[1024]{0:T(1024)S(1)} %bitcast.225), kind=kOutput, calls=%fused_computation.12 | convolution fusion | flops 543162368 | bytes 1589248 | tf_op jit(solution)/shard_map/dot_general | solution.py:127
  98.9 2.3 %fusion.2 = f32[1024,256]{0,1:T(8,128)S(1)} fusion(bf16[1024,256]{0,1:T(8,128)(2,1)S(1)} %get-tuple-element.8, f32[1024]{0:T(1024)S(1)} %bitcast.245, s32[1024]{0:T(1024)S(1)} %bitcast.241, f32[1024]{0:T(1024)S(1)} %bitcast.247, s32[1024]{0:T(1024)S(1)} %bitcast.243), kind=kOutput, calls=%fused_computation.14 | convolution fusion | flops 543162368 | bytes 1589248 | tf_op jit(solution)/shard_map/dot_general | solution.py:127
  101.2 2.3 %fusion.6 = f32[1024,256]{0,1:T(8,128)S(1)} fusion(bf16[1024,256]{0,1:T(8,128)(2,1)S(1)} %get-tuple-element.8, f32[1024]{0:T(1024)S(1)} %bitcast.221, s32[1024]{0:T(1024)S(1)} %bitcast.217, f32[1024]{0:T(1024)S(1)} %bitcast.223, s32[1024]{0:T(1024)S(1)} %bitcast.219), kind=kOutput, calls=%fused_computation.18 | convolution fusion | flops 543162368 | bytes 1589248 | tf_op jit(solution)/shard_map/dot_general | solution.py:127
  103.5 1.9 %add_multiply_fusion = f32[1024,256]{0,1:T(8,128)S(1)} fusion(f32[1024,256]{0,1:T(8,128)S(1)} %get-tuple-element.9, f32[1024,256]{0,1:T(8,128)S(1)} %fusion.6, f32[1024,256]{0,1:T(8,128)S(1)} %fusion, f32[1024,256]{0,1:T(8,128)S(1)} %fusion.2, f32[1024]{0:T(1024)S(1)} %copy-done.39, f32[256]{0:T(256)S(1)} %convert_element_type.49, ...), kind=kOutput, calls=%fused_computation.40 | convolution fusion | flops 546570240 | bytes 5788672 | tf_op jit(solution)/shard_map/dot_general | solution.py:127
  105.7 7.4 %collective-permute-start.13 = (f32[128,256]{0,1:T(8,128)S(1)}, f32[128,256]{0,1:T(8,128)S(1)}, u32[]{:S(2)}, u32[]{:S(2)}) collective-permute-start(f32[128,256]{0,1:T(8,128)S(1)} %convolution_bitcast_fusion), channel_id=1, source_target_pairs={{1,0},{2,1},{3,2},{4,3},{5,4},{6,5},{7,6},{8,7},{9,8},{10,9},{11,1... | collective-permute-start | bytes 393224 | tf_op jit(solution)/shard_map/ppermute | solution.py:46
  114.5 2.8 %collective-permute-done.12 = f32[128,256]{0,1:T(8,128)S(1)} collective-permute-done((f32[128,256]{0,1:T(8,128)S(1)}, f32[128,256]{0,1:T(8,128)S(1)}, u32[]{:S(2)}, u32[]{:S(2)}) %collective-permute-start.12) | collective-permute-done | bytes 131104 | tf_op jit(solution)/shard_map/ppermute | solution.py:44
  (147 shorter events, 19.6 us)
Async XLA Ops:
  0.6 55.2 %copy-start = (bf16[128,1024]{1,0:T(8,128)(2,1)S(1)}, bf16[128,1024]{1,0:T(8,128)(2,1)}, u32[]{:S(2)}) copy-start(bf16[128,1024]{1,0:T(8,128)(2,1)} %param.23) | copy-start | bytes 786436
  2.2 25.1 %copy-start.15 = (f32[4,256]{1,0:T(4,128)S(1)}, f32[4,256]{1,0:T(4,128)}, u32[]{:S(2)}) copy-start(f32[4,256]{1,0:T(4,128)} %param.25) | copy-start | bytes 12292
  2.2 25.7 %copy-start.13 = (f32[2,1024]{1,0:T(2,128)S(1)}, f32[2,1024]{1,0:T(2,128)}, u32[]{:S(2)}) copy-start(f32[2,1024]{1,0:T(2,128)} %param.18) | copy-start | bytes 24580
  2.2 25.7 %copy-start.9 = (s32[2,1024]{1,0:T(2,128)S(1)}, s32[2,1024]{1,0:T(2,128)}, u32[]{:S(2)}) copy-start(s32[2,1024]{1,0:T(2,128)} %param.19) | copy-start | bytes 24580
  2.2 33.1 %collective-permute-start = (f32[2,128]{1,0:T(2,128)}, f32[2,128]{1,0:T(2,128)}, u32[]{:S(2)}, u32[]{:S(2)}) collective-permute-start(f32[2,128]{1,0:T(2,128)} %multiply_reduce_fusion), channel_id=1, source_target_pairs={{0,1},{1,2},{2,3},{3,4},{4,5},{5,6},{6,7},{7,8},{8,9},{9,10},{10,1... | collective-permute-start | bytes 3080 | tf_op jit(solution)/shard_map/ppermute | solution.py:25
  4.8 32.1 %collective-permute-start.1 = (f32[2,128]{1,0:T(2,128)}, f32[2,128]{1,0:T(2,128)}, u32[]{:S(2)}, u32[]{:S(2)}) collective-permute-start(f32[2,128]{1,0:T(2,128)} %multiply_reduce_fusion), channel_id=1, source_target_pairs={{1,0},{2,1},{3,2},{4,3},{5,4},{6,5},{7,6},{8,7},{9,8},{10,9},{11,1... | collective-permute-start | bytes 3080 | tf_op jit(solution)/shard_map/ppermute | solution.py:26
  15.6 30.5 %collective-permute-start.2 = (f32[1024,1,256]{0,2,1:T(8,128)S(1)}, f32[1024,1,256]{0,2,1:T(8,128)S(1)}, u32[]{:S(2)}, u32[]{:S(2)}) collective-permute-start(f32[1024,1,256]{0,2,1:T(8,128)S(1)} %bitcast.194), channel_id=1, source_target_pairs={{0,1},{1,2},{2,3},{3,4},{4,5},{5,6},{6,7},{7,8},{8,9},{9,10},{10,1... | collective-permute-start | bytes 3145736 | tf_op jit(solution)/shard_map/ppermute | solution.py:25
  15.7 30.4 %collective-permute-start.3 = (f32[1024,1,256]{0,2,1:T(8,128)S(1)}, f32[1024,1,256]{0,2,1:T(8,128)S(1)}, u32[]{:S(2)}, u32[]{:S(2)}) collective-permute-start(f32[1024,1,256]{0,2,1:T(8,128)S(1)} %bitcast.195), channel_id=1, source_target_pairs={{1,0},{2,1},{3,2},{4,3},{5,4},{6,5},{7,6},{8,7},{9,8},{10,9},{11,1... | collective-permute-start | bytes 3145736 | tf_op jit(solution)/shard_map/ppermute | solution.py:26
  23.4 49.3 %collective-permute-start.6 = (f32[64,1,128]{2,0,1:T(8,128)}, f32[64,1,128]{2,0,1:T(8,128)}, u32[]{:S(2)}, u32[]{:S(2)}) collective-permute-start(f32[64,1,128]{2,0,1:T(8,128)} %get-tuple-element.23), channel_id=1, source_target_pairs={{1,0},{2,1},{3,2},{4,3},{5,4},{6,5},{7,6},{8,7},{9,8},{10,9},{11,1... | collective-permute-start | bytes 98312 | tf_op jit(solution)/shard_map/ppermute | solution.py:26
  31.4 40.5 %copy-start.31 = (s32[128]{0:T(128)}, s32[128]{0:T(128)S(1)}, u32[]{:S(2)}) copy-start(s32[128]{0:T(128)S(1)} %get-tuple-element.86) | copy-start | bytes 1540
  31.4 40.5 %copy-start.33 = (s32[128]{0:T(128)}, s32[128]{0:T(128)S(1)}, u32[]{:S(2)}) copy-start(s32[128]{0:T(128)S(1)} %get-tuple-element.87) | copy-start | bytes 1540
  31.4 40.5 %copy-start.35 = (s32[128]{0:T(128)}, s32[128]{0:T(128)S(1)}, u32[]{:S(2)}) copy-start(s32[128]{0:T(128)S(1)} %get-tuple-element.88) | copy-start | bytes 1540
  31.4 40.5 %copy-start.37 = (s32[128]{0:T(128)}, s32[128]{0:T(128)S(1)}, u32[]{:S(2)}) copy-start(s32[128]{0:T(128)S(1)} %get-tuple-element.89) | copy-start | bytes 1540
  35.3 37.5 %collective-permute-start.7 = (f32[64,1,128]{2,0,1:T(8,128)}, f32[64,1,128]{2,0,1:T(8,128)S(1)}, u32[]{:S(2)}, u32[]{:S(2)}) collective-permute-start(f32[64,1,128]{2,0,1:T(8,128)} %get-tuple-element.23), channel_id=1, source_target_pairs={{0,1},{1,2},{2,3},{3,4},{4,5},{5,6},{6,7},{7,8},{8,9},{9,10},{10,1... | collective-permute-start | bytes 98312 | tf_op jit(solution)/shard_map/ppermute | solution.py:25
  56.2 11.4 %collective-permute-start.4 = (f32[128,256]{0,1:T(8,128)S(1)}, f32[128,256]{0,1:T(8,128)S(1)}, u32[]{:S(2)}, u32[]{:S(2)}) collective-permute-start(f32[128,256]{0,1:T(8,128)S(1)} %convolution_bitcast_fusion.1), channel_id=1, source_target_pairs={{0,1},{1,2},{2,3},{3,4},{4,5},{5,6},{6,7},{7,8},{8,9},{9,10},{10,1... | collective-permute-start | bytes 393224 | tf_op jit(solution)/shard_map/ppermute | solution.py:44
  56.2 15.6 %collective-permute-start.5 = (f32[128,256]{0,1:T(8,128)S(1)}, f32[128,256]{0,1:T(8,128)S(1)}, u32[]{:S(2)}, u32[]{:S(2)}) collective-permute-start(f32[128,256]{0,1:T(8,128)S(1)} %convolution_bitcast_fusion.1), channel_id=1, source_target_pairs={{1,0},{2,1},{3,2},{4,3},{5,4},{6,5},{7,6},{8,7},{9,8},{10,9},{11,1... | collective-permute-start | bytes 393224 | tf_op jit(solution)/shard_map/ppermute | solution.py:46
  64.5 31.1 %collective-permute-start.10 = (f32[1024,1,256]{0,2,1:T(8,128)S(1)}, f32[1024,1,256]{0,2,1:T(8,128)S(1)}, u32[]{:S(2)}, u32[]{:S(2)}) collective-permute-start(f32[1024,1,256]{0,2,1:T(8,128)S(1)} %bitcast.199), channel_id=1, source_target_pairs={{0,1},{1,2},{2,3},{3,4},{4,5},{5,6},{6,7},{7,8},{8,9},{9,10},{10,1... | collective-permute-start | bytes 3145736 | tf_op jit(solution)/shard_map/ppermute | solution.py:25
  67.5 28.1 %collective-permute-start.11 = (f32[1024,1,256]{0,2,1:T(8,128)S(1)}, f32[1024,1,256]{0,2,1:T(8,128)S(1)}, u32[]{:S(2)}, u32[]{:S(2)}) collective-permute-start(f32[1024,1,256]{0,2,1:T(8,128)S(1)} %bitcast.201), channel_id=1, source_target_pairs={{1,0},{2,1},{3,2},{4,3},{5,4},{6,5},{7,6},{8,7},{9,8},{10,9},{11,1... | collective-permute-start | bytes 3145736 | tf_op jit(solution)/shard_map/ppermute | solution.py:26
  74.0 21.1 %collective-permute-start.8 = (f32[2,128]{1,0:T(2,128)S(1)}, f32[2,128]{1,0:T(2,128)S(1)}, u32[]{:S(2)}, u32[]{:S(2)}) collective-permute-start(f32[2,128]{1,0:T(2,128)S(1)} %fusion.73), channel_id=1, source_target_pairs={{0,1},{1,2},{2,3},{3,4},{4,5},{5,6},{6,7},{7,8},{8,9},{9,10},{10,1... | collective-permute-start | bytes 3080 | tf_op jit(solution)/shard_map/ppermute | solution.py:25
  74.1 21.0 %collective-permute-start.9 = (f32[2,128]{1,0:T(2,128)S(1)}, f32[2,128]{1,0:T(2,128)S(1)}, u32[]{:S(2)}, u32[]{:S(2)}) collective-permute-start(f32[2,128]{1,0:T(2,128)S(1)} %fusion.73), channel_id=1, source_target_pairs={{1,0},{2,1},{3,2},{4,3},{5,4},{6,5},{7,6},{8,7},{9,8},{10,9},{11,1... | collective-permute-start | bytes 3080 | tf_op jit(solution)/shard_map/ppermute | solution.py:26
  81.4 36.9 %collective-permute-start.14 = (f32[64,1,128]{2,0,1:T(8,128)S(1)}, f32[64,1,128]{2,0,1:T(8,128)S(1)}, u32[]{:S(2)}, u32[]{:S(2)}) collective-permute-start(f32[64,1,128]{2,0,1:T(8,128)S(1)} %get-tuple-element.10), channel_id=1, source_target_pairs={{1,0},{2,1},{3,2},{4,3},{5,4},{6,5},{7,6},{8,7},{9,8},{10,9},{11,1... | collective-permute-start | bytes 98312 | tf_op jit(solution)/shard_map/ppermute | solution.py:26
  95.1 23.2 %collective-permute-start.15 = (f32[64,1,128]{2,0,1:T(8,128)S(1)}, f32[64,1,128]{2,0,1:T(8,128)S(1)}, u32[]{:S(2)}, u32[]{:S(2)}) collective-permute-start(f32[64,1,128]{2,0,1:T(8,128)S(1)} %get-tuple-element.10), channel_id=1, source_target_pairs={{0,1},{1,2},{2,3},{3,4},{4,5},{5,6},{6,7},{7,8},{8,9},{9,10},{10,1... | collective-permute-start | bytes 98312 | tf_op jit(solution)/shard_map/ppermute | solution.py:25
  105.6 11.7 %collective-permute-start.12 = (f32[128,256]{0,1:T(8,128)S(1)}, f32[128,256]{0,1:T(8,128)S(1)}, u32[]{:S(2)}, u32[]{:S(2)}) collective-permute-start(f32[128,256]{0,1:T(8,128)S(1)} %convolution_bitcast_fusion), channel_id=1, source_target_pairs={{0,1},{1,2},{2,3},{3,4},{4,5},{5,6},{6,7},{7,8},{8,9},{9,10},{10,1... | collective-permute-start | bytes 393224 | tf_op jit(solution)/shard_map/ppermute | solution.py:44
  105.7 11.6 %collective-permute-start.13 = (f32[128,256]{0,1:T(8,128)S(1)}, f32[128,256]{0,1:T(8,128)S(1)}, u32[]{:S(2)}, u32[]{:S(2)}) collective-permute-start(f32[128,256]{0,1:T(8,128)S(1)} %convolution_bitcast_fusion), channel_id=1, source_target_pairs={{1,0},{2,1},{3,2},{4,3},{5,4},{6,5},{7,6},{8,7},{9,8},{10,9},{11,1... | collective-permute-start | bytes 393224 | tf_op jit(solution)/shard_map/ppermute | solution.py:46
  (32 other events, 189.0 us)
where the time goes:
time: 120 us; the launch traced here: 119 us
  starting transfers between devices  47.8 us (40%)
  waiting for transfers between devices  27.3 us (23%)
  matrix products  21.5 us (18%)
  local copies, waits for them, and re-layouts  15 us (12%)
  other arithmetic  6.05 us (5%)
  between operations  1.41 us (1%)
    ppermute x6, starting transfers between devices, padded_2(): lax.ppermute(first, axis, [(b, a) for a, b in up])  27.9 us
    ppermute x6, waiting for transfers between devices, padded_2(): lax.ppermute(last, axis, up)  21.5 us
    dot_general x8, matrix products, sources(): jnp.dot(quad_tables[config], rounded, preferred_element_type=jnp.float32)  17.6 us
    ppermute x2, starting transfers between devices, padded_3(): lax.ppermute(head, axis, [((i + 1) % count, i) for i in range(count)])  15.3 us
    ppermute x2, waiting for transfers between devices, padded_3(): lax.ppermute(tail, axis, [(i, (i + 1) % count) for i in range(count)])  5.74 us
    ppermute x6, starting transfers between devices, padded_2(): lax.ppermute(last, axis, up)  4.38 us
    unnamed x83, local copies, waits for them, and re-layouts  3.97 us
  transfers between devices with their start and end apart: 16, of which 4 were waited for; matrix products, arithmetic and copies ran while one was open for 33% of the time, Pallas kernels for 0%

commit v1 on v0

v1 whole, which is shorter than its diff:
```python
import functools

import jax
import jax.numpy as jnp
from jax import lax
from jax.experimental import pallas as pl
from jax.experimental.pallas import tpu as pltpu
from jax.sharding import PartitionSpec as P

K = 1024
L = 64
MX = 256
OX = 128
AXES = ("mp", "dev")
EXTRA = 40
FAST = 576
F32 = jnp.float32
BF16 = jnp.bfloat16
VMEM = pl.BlockSpec(memory_space=pltpu.VMEM)
SMEM = pl.BlockSpec(memory_space=pltpu.SMEM)
HIGHEST = lax.Precision.HIGHEST


def dot_nt(a, b):
    return lax.dot_general(a, b, (((1,), (1,)), ((), ())), preferred_element_type=F32)


def dot_nn(a, b):
    return jnp.dot(a, b, preferred_element_type=F32)


def dot_exact(a, b):
    return jnp.dot(a, b, precision=HIGHEST, preferred_element_type=F32)


def split3(x):
    high = x.astype(BF16)
    rest = x - high.astype(F32)
    middle = rest.astype(BF16)
    low = (rest - middle.astype(F32)).astype(BF16)
    return high, middle, low


def one_hot_rows(select_ref, pos_ref):
    place = lax.broadcasted_iota(jnp.int32, (K, 128), 0).astype(F32)
    for block in range(8):
        hit = place == pos_ref[block : block + 1, :]
        select_ref[:, block * 128 : (block + 1) * 128] = jnp.where(hit, 1.0, 0.0).astype(BF16)


def pack_kernel(
    count, sign, spectrum, currents, level, ocean_index, ocean_weight,
    up, down, pos, surface, select, parts,
):
    for block in range(8):
        pos[block : block + 1, :] = sign[1:2, block * 128 : (block + 1) * 128].astype(F32)
    ones = pos[...]
    upper = lax.broadcasted_iota(jnp.int32, (128, 128), 0) <= lax.broadcasted_iota(
        jnp.int32, (128, 128), 1
    )
    before = dot_nn(ones.astype(BF16), jnp.where(upper, 1.0, 0.0).astype(BF16))
    running = jnp.zeros((1, 1), F32)
    counts = []
    for block in range(8):
        counts.append(before[block : block + 1, :] + running)
        running = running + before[block : block + 1, 127:128]
    lane = lax.broadcasted_iota(jnp.int32, (1, 128), 1).astype(F32)
    for block in range(8):
        index = lane + float(block * 128)
        first = counts[block] - 1.0
        second = running + index - counts[block]
        pos[block : block + 1, :] = jnp.where(ones[block : block + 1, :] > 0.5, first, second)
    one_hot_rows(select, pos)
    high, middle, low = split3(spectrum[...])
    parts[:, 0:MX] = high
    parts[:, MX : 2 * MX] = middle
    parts[:, 2 * MX : 3 * MX] = low
    for block in range(4):
        rows = slice(block * 256, (block + 1) * 256)
        got = dot_nn(select[rows, :], parts[...])
        value = got[:, 0:MX] + (got[:, MX : 2 * MX] + got[:, 2 * MX :])
        top = min((block + 1) * 256, count)
        if top > block * 256:
            up[block * 256 : top, :] = value[: top - block * 256]
        skip = K - count
        start = max(block * 256, skip)
        if start < (block + 1) * 256:
            down[start - skip : (block + 1) * 256 - skip, :] = value[start - block * 256 :]
    weights = jnp.broadcast_to(level[...], (8, L))
    flat_u = dot_exact(weights, currents[0])
    flat_v = dot_exact(weights, currents[1])
    surface[...] = flat_u
    surface[1:2, :] = flat_v[0:1, :]
    for message in (up, down):
        message[count : count + 1, 0:OX] = flat_u[0:1, :]
        message[count : count + 1, OX : 2 * OX] = flat_v[0:1, :]
        message[count + 1 : count + 5, 0:OX] = ocean_index[...].astype(F32)
        message[count + 1 : count + 5, OX : 2 * OX] = ocean_weight[...]
        message[count + 5 : count + 8, :] = jnp.zeros((3, MX), F32)
        message[count + 8 : count + 40, 0:OX] = currents[0, 0 : L // 2, :]
        message[count + 8 : count + 40, OX : 2 * OX] = currents[0, L // 2 :, :]


def table_kernel(
    row, pos, sign, courant, nonlinear, quad_index, quad_weight, stokes_table, point_index,
    point_weight, quad, back, stokes_sorted, wide, spread, select, rows, parts,
):
    one_hot_rows(select, pos)
    sense = (2 * sign[...] - 1).astype(F32)
    speed = courant[...]
    rows[...] = jnp.zeros((32, K), F32)
    rows[0:2, :] = speed
    rows[2:4, :] = 0.5 * speed * sense
    rows[4:6, :] = sense
    rows[6:7, :] = nonlinear[...]
    for config in range(4):
        index = quad_index[config]
        weight = quad_weight[config]
        same = index[0:1] == index[1:2]
        first = jnp.where(same, weight[0:1] + weight[1:2], weight[0:1])
        second = jnp.where(same, 0.0, weight[1:2])
        rows[8 + 2 * config : 9 + 2 * config, :] = first.astype(BF16).astype(F32)
        rows[9 + 2 * config : 10 + 2 * config, :] = second.astype(BF16).astype(F32)
        rows[16 + 2 * config : 18 + 2 * config, :] = index.astype(F32)
    high, middle, low = split3(rows[...])
    parts[0:32, :] = high
    parts[32:64, :] = middle
    parts[64:96, :] = low
    component = lax.broadcasted_iota(jnp.int32, (16, K), 1)
    line = lax.broadcasted_iota(jnp.int32, (16, K), 0)
    digits = jnp.where(line == 0, component // 32, component % 32).astype(F32).astype(BF16)
    found = dot_nt(digits, select[...])
    order = found[0:1] * 32.0 + found[1:2]
    stokes_sorted[...] = dot_nt(stokes_table[...], select[...]).astype(BF16)

    def block_rows(block, carry):
        at = pl.ds(pl.multiple_of(block * 64, 64), 64)
        got = dot_nt(select[at, :], parts[...])
        column = got[:, 0:32] + (got[:, 32:64] + got[:, 64:96])
        for item in range(7):
            wide[item, at, :] = jnp.broadcast_to(column[:, item : item + 1], (64, 128))
        original = (lax.broadcasted_iota(jnp.int32, (64, K), 0) + block * 64).astype(F32)
        back[at, :] = jnp.where(order == original, 1.0, 0.0).astype(BF16)
        for config in range(4):
            a = 8 + 2 * config
            b = 16 + 2 * config
            value = jnp.where(
                order == column[:, b : b + 1],
                column[:, a : a + 1],
                jnp.where(order == column[:, b + 1 : b + 2], column[:, a + 1 : a + 2], 0.0),
            )
            quad[config, at, :] = value.astype(BF16)
        return carry

    lax.fori_loop(0, K // 64, block_rows, 0)
    here = row[0]
    for shift in range(3):
        base = ((here + (shift + 255)) % 256) * OX
        slot = lax.broadcasted_iota(jnp.int32, (OX, MX), 0) + base
        total = jnp.zeros((OX, MX), F32)
        for config in range(4):
            total = total + jnp.where(
                point_index[config : config + 1, :] == slot, point_weight[config : config + 1, :], 0.0
            )
        spread[shift * OX : (shift + 1) * OX, :] = total


def cell_table(base, index, weight):
    point = (lax.broadcasted_iota(jnp.int32, (MX, OX), 0) + base).astype(F32)
    total = jnp.zeros((MX, OX), F32)
    for config in range(4):
        total = total + jnp.where(
            index[config : config + 1, :] == point, weight[config : config + 1, :], 0.0
        )
    return total


def update(count, own_up, own_down, from_below, from_above, flow, quad, wide, stokes_sorted, wet,
           write, advected, rounded, finished):
    bend = jnp.tanh(flow)
    bend_x = bend[0:1, :]
    bend_y = bend[1:2, :]
    skip = K - count
    size = 32

    def advect(start, own, shift, behind):
        def body(block, carry):
            at = pl.multiple_of(block * size + start, size)
            here = own[pl.ds(at - shift, size), :]
            west = pltpu.roll(here, 1, 1)
            east = pltpu.roll(here, MX - 1, 1)

            def both(item):
                half = wide[item, pl.ds(at, size), :]
                return jnp.concatenate([half, half], axis=1)

            behind_x = jnp.where(both(4) > 0.0, west, east)
            speed_x = both(0) + both(2) * bend_x
            speed_y = both(1) + both(3) * bend_y
            value = here - speed_x * (here - behind_x) - speed_y * (here - behind(at, both))
            advected[pl.ds(at, size), :] = value
            rounded[pl.ds(at, size), :] = value.astype(BF16)
            return carry

        return body

    def below(at, both):
        return from_below[pl.ds(at, size), :]

    def above(at, both):
        return from_above[pl.ds(at - skip, size), :]

    def either(at, both):
        return jnp.where(both(5) > 0.0, below(at, both), above(at, both))

    if skip:
        lax.fori_loop(0, skip // size, advect(0, own_up, 0, below), 0)
    lax.fori_loop(0, (count - skip) // size, advect(skip, own_up, 0, either), 0)
    if skip:
        lax.fori_loop(0, skip // size, advect(count, own_down, skip, above), 0)

    def source(block, carry):
        at = pl.ds(pl.multiple_of(block * 64, 64), 64)
        interp = [dot_nn(quad[config, at, :], rounded[...]) for config in range(4)]
        value = advected[at, :]
        pairs = interp[0] * interp[1] + interp[2] * interp[3]
        total = (interp[0] + interp[1]) + (interp[2] + interp[3])
        gain = wide[6, at, :]
        gain = jnp.concatenate([gain, gain], axis=1)
        result = wet * (value + gain * (value * (value * total - pairs)))
        advected[at, :] = result
        finished[at, :] = result.astype(BF16)
        return carry

    lax.fori_loop(0, K // 64, source, 0)
    write(advected)
    return dot_nn(stokes_sorted[...], finished[...])


def flow_of(below_surface, own_surface, above_surface, spread):
    wide_u = jnp.concatenate([below_surface[0], own_surface[0], above_surface[0]], axis=1)
    wide_v = jnp.concatenate([below_surface[1], own_surface[1], above_surface[1]], axis=1)
    line = lax.broadcasted_iota(jnp.int32, (8, 3 * OX), 0)
    both = jnp.where(line == 0, wide_u, wide_v)
    return dot_exact(both, spread[...])


def first_kernel(
    count, row, own_up, own_down, from_below, from_above, surface, quad, wide, stokes_sorted, spread,
    wet, ocean_index, ocean_weight, up, down, to_below, own_part, to_above, cells,
    advected, rounded, finished,
):
    base = row[0] * MX
    cells[:, 0:OX] = cell_table(
        base, from_below[count + 1 : count + 5, 0:OX], from_below[count + 1 : count + 5, OX:]
    )
    cells[:, OX : 2 * OX] = cell_table(base, ocean_index[...].astype(F32), ocean_weight[...])
    cells[:, 2 * OX :] = cell_table(
        base, from_above[count + 1 : count + 5, 0:OX], from_above[count + 1 : count + 5, OX:]
    )
    sides = [
        (message[count : count + 1, 0:OX], message[count : count + 1, OX:])
        for message in (from_below, from_above)
    ]
    flow = flow_of(sides[0], (surface[0:1, :], surface[1:2, :]), sides[1], spread)

    def write(result):
        up[...] = result[0:count, :]
        down[...] = result[K - count :, :]

    stokes = update(count, own_up, own_down, from_below, from_above, flow, quad, wide, stokes_sorted,
                    wet[...], write, advected, rounded, finished)
    part = dot_exact(stokes, cells[...])
    to_below[...] = part[:, 0:OX]
    own_part[...] = part[:, OX : 2 * OX]
    to_above[...] = part[:, 2 * OX :]


def second_kernel(
    count, own_up, own_down, from_below, from_above, ocean_below, ocean_own, ocean_above, quad, wide,
    stokes_sorted, spread, wet, cells, spectra, to_below, own_part, to_above,
    advected, rounded, finished,
):
    sides = [
        (message[L : L + 1, :], message[L + 1 : L + 2, :])
        for message in (ocean_below, ocean_own, ocean_above)
    ]
    flow = flow_of(sides[0], sides[1], sides[2], spread)

    def write(result):
        spectra[...] = result[...]

    stokes = update(count, own_up, own_down, from_below, from_above, flow, quad, wide, stokes_sorted,
                    wet[...], write, advected, rounded, finished)
    part = dot_exact(stokes, cells[...])
    to_below[...] = part[:, 0:OX]
    own_part[...] = part[:, OX : 2 * OX]
    to_above[...] = part[:, 2 * OX :]


def restore_kernel(spectra, back, out):
    high, middle, low = split3(spectra[...])
    out[...] = dot_nn(back[...], high) + (dot_nn(back[...], middle) + dot_nn(back[...], low))


def mix(profile, mixing):
    line = lax.broadcasted_iota(jnp.int32, (L, OX), 0)
    before = jnp.where(line == 0, profile, pltpu.roll(profile, 1, 0))
    after = jnp.where(line == L - 1, profile, pltpu.roll(profile, L - 1, 0))
    return mixing * (before - 2.0 * profile + after)


def ocean_step(u, v, u_below, u_above, drift, rotation, mixing):
    vorticity = 0.5 * (pltpu.roll(v, OX - 1, 1) - pltpu.roll(v, 1, 1)) - 0.5 * (u_above - u_below)
    drift_x = drift[0:L, :]
    drift_y = drift[L:, :]
    new_u = u + 0.5 * (rotation * (v + drift_y) + vorticity * drift_y + mix(u, mixing))
    new_v = v + 0.5 * (-rotation * (u + drift_x) - vorticity * drift_x + mix(v, mixing))
    return new_u, new_v


def first_ocean(
    count, currents, from_below, from_above, part_below, own_part, part_above, coriolis, mixing, level,
    state, message,
):
    half = L // 2

    def zonal(block):
        rows = block[count + 8 : count + 40, :]
        return jnp.concatenate([rows[0:half, 0:OX], rows[0:half, OX:]], axis=0)

    drift = own_part[...] + part_below[...] + part_above[...]
    new_u, new_v = ocean_step(
        currents[0], currents[1], zonal(from_below), zonal(from_above), drift, coriolis[...], mixing[...]
    )
    state[0] = new_u
    state[1] = new_v
    weights = jnp.broadcast_to(level[...], (8, L))
    message[0:L, :] = new_u
    message[L:, :] = dot_exact(weights, new_u)
    message[L + 1 : L + 2, :] = dot_exact(weights, new_v)[0:1, :]


def second_ocean(
    state, ocean_below, ocean_above, part_below, own_part, part_above, coriolis, mixing, out
):
    drift = own_part[...] + part_below[...] + part_above[...]
    new_u, new_v = ocean_step(
        state[0], state[1], ocean_below[0:L, :], ocean_above[0:L, :], drift, coriolis[...], mixing[...]
    )
    out[0] = new_u
    out[1] = new_v


def shape(*dims, dtype=F32):
    return jax.ShapeDtypeStruct(dims, dtype)


def call(body, outs, scratch=(), scalars=0, inputs=0, flops=0, data=0, name=None):
    return pl.pallas_call(
        body,
        out_shape=outs,
        in_specs=[SMEM] * scalars + [VMEM] * (inputs - scalars),
        out_specs=jax.tree.map(lambda _: VMEM, outs),
        scratch_shapes=scratch,
        cost_estimate=pl.CostEstimate(flops=flops, bytes_accessed=data, transcendentals=0),
        compiler_params=pltpu.CompilerParams(vmem_limit_bytes=40 << 20),
        name=name,
    )


def exchange(to_above, to_below):
    total = lax.axis_size("mp") * lax.axis_size("dev")
    up = [(i, (i + 1) % total) for i in range(total)]
    return (
        lax.ppermute(to_above, AXES, up),
        lax.ppermute(to_below, AXES, [(b, a) for a, b in up]),
    )


def program(
    count, row, spectrum, wet, courant, stencil_sign, quad_index, quad_weight, nonlinear, stokes_table,
    point_index, point_weight, ocean_index, ocean_weight, currents, coriolis, mixing, level,
):
    part = shape(128, OX)
    work = (pltpu.VMEM((K, MX), F32), pltpu.VMEM((K, MX), BF16), pltpu.VMEM((K, MX), BF16))
    up, down, pos, surface = call(
        functools.partial(pack_kernel, count),
        (shape(count + EXTRA, MX), shape(count + EXTRA, MX), shape(8, 128), shape(8, 128)),
        (pltpu.VMEM((K, K), BF16), pltpu.VMEM((K, 3 * MX), BF16)),
        inputs=6, flops=2 * K * K * 3 * MX, data=1 << 20, name="pack",
    )(stencil_sign, spectrum, currents, level, ocean_index, ocean_weight)
    below, above = exchange(up, down)
    quad, back, stokes_sorted, wide, spread = call(
        table_kernel,
        (
            shape(4, K, K, dtype=BF16), shape(K, K, dtype=BF16), shape(128, K, dtype=BF16),
            shape(7, K, 128), shape(3 * OX, MX),
        ),
        (pltpu.VMEM((K, K), BF16), pltpu.VMEM((32, K), F32), pltpu.VMEM((96, K), BF16)),
        scalars=1, inputs=10, flops=8 << 30, data=12 << 20, name="tables",
    )(row, pos, stencil_sign, courant, nonlinear, quad_index, quad_weight, stokes_table, point_index,
      point_weight)
    up, down, to_below, own_part, to_above, cells = call(
        functools.partial(first_kernel, count),
        (shape(count, MX), shape(count, MX), part, part, part, shape(MX, 3 * OX)),
        work, scalars=1, inputs=13, flops=3 << 30, data=12 << 20, name="first",
    )(row, up, down, below, above, surface, quad, wide, stokes_sorted, spread, wet, ocean_index,
      ocean_weight)
    part_below, part_above = exchange(to_above, to_below)
    next_below, next_above = exchange(up, down)
    state, message = call(
        functools.partial(first_ocean, count),
        (shape(2, L, OX), shape(L + 8, OX)),
        inputs=9, flops=1 << 20, data=1 << 18, name="ocean",
    )(currents, below, above, part_below, own_part, part_above, coriolis, mixing, level)
    ocean_below, ocean_above = exchange(message, message)
    spectra, to_below, own_part, to_above = call(
        functools.partial(second_kernel, count),
        (shape(K, MX), part, part, part),
        work, inputs=13, flops=3 << 30, data=12 << 20, name="second",
    )(up, down, next_below, next_above, ocean_below, message, ocean_above, quad, wide, stokes_sorted,
      spread, wet, cells)
    part_below, part_above = exchange(to_above, to_below)
    out = call(
        restore_kernel, shape(K, MX), inputs=2, flops=2 * K * K * 3 * MX, data=4 << 20, name="restore",
    )(spectra, back)
    final = call(
        second_ocean, shape(2, L, OX), inputs=8, flops=1 << 20, data=1 << 18, name="ocean_end",
    )(state, ocean_below, ocean_above, part_below, own_part, part_above, coriolis, mixing)
    return out, final


def local(
    spectrum, water_mask, courant, stencil_sign, quad_index, quad_weight, nonlinear, stokes_table,
    point_index, point_weight, ocean_index, ocean_weight, currents, coriolis, mixing, surface_weights,
):
    row = (lax.axis_index("mp") * lax.axis_size("dev") + lax.axis_index("dev")).reshape(1)
    arguments = (
        row.astype(jnp.int32),
        spectrum,
        water_mask.astype(F32).reshape(1, MX),
        courant,
        stencil_sign,
        quad_index.transpose(0, 2, 1),
        quad_weight.transpose(0, 2, 1),
        nonlinear.reshape(1, K),
        stokes_table,
        point_index,
        point_weight,
        ocean_index,
        ocean_weight,
        currents,
        coriolis.reshape(1, OX),
        jnp.broadcast_to(mixing[:, None], (L, OX)),
        surface_weights.reshape(1, L),
    )
    northward = jnp.sum(stencil_sign[1])
    balanced = jnp.logical_and(northward <= FAST, K - northward <= FAST)
    return lax.cond(
        balanced, functools.partial(program, FAST), functools.partial(program, K), *arguments
    )


def solution(mesh):
    whole = P(AXES)
    last = P(None, AXES)
    return jax.shard_map(
        local,
        mesh=mesh,
        in_specs=(
            last, whole, P(), P(), P(), P(), P(), P(), last, last, last, last,
            P(None, None, AXES), whole, P(), P(),
        ),
        out_specs=(last, P(None, None, AXES)),
        check_vma=False,
    )
```

time: 120 us -> 109 us (0.908)
  Pallas kernels: 0 us -> 53.7 us
  matrix products: 21.5 us -> 0 us
  waiting for transfers between devices: 27.3 us -> 8.7 us
  local copies, waits for them, and re-layouts: 15 us -> 0.16 us
  starting transfers between devices: 47.8 us -> 42.1 us
  other arithmetic: 6.05 us -> 2.02 us
    pallas_call x0 -> x7, Pallas kernels: none -> 53.7 us  [the longest x1 15.6 us: program(): call(functools.partial(first_kernel, count), (shape(count, MX), shape(cou...]
    dot_general x14 -> x0, matrix products: 21.5 us -> none  [the longest x8 17.6 us: sources(): jnp.dot(quad_tables[config], rounded, preferred_element_type=jnp.float32)]
    ppermute x16 -> x10, waiting for transfers between devices: 27.3 us -> 8.7 us  [the longest x5 8.58 us: exchange(): lax.ppermute(to_above, AXES, up)]
    ppermute x16 -> x10, starting transfers between devices: 47.8 us -> 42.1 us  [the longest x5 39.5 us: exchange(): lax.ppermute(to_below, AXES, [(b, a) for a, b in up])]
    slice x17 -> x0, local copies, waits for them, and re-layouts: 5.18 us -> none  [the longest x4 2.39 us: quad_table(): first_part = jnp.where(row_index[:, 0:1] == columns, weight[:, 0:1], 0.0)]
    unnamed x83 -> x0, local copies, waits for them, and re-layouts: 3.97 us -> none
    squeeze x2 -> x0, local copies, waits for them, and re-layouts: 2.71 us -> none  [the longest x1 1.36 us: local(): quad_index[config]]
    concatenate x5 -> x0, local copies, waits for them, and re-layouts: 1.67 us -> none  [the longest x4 1.04 us: advect(): jnp.roll(spectra, 1, axis=2)]
  transfers between devices with their start and end apart: 16 -> 10, of which waited for: 4 -> 3; matrix products, arithmetic and copies ran while one was open for 33% -> 0% of each run, Pallas kernels for 0% -> 17%
where the time goes in v1:
time: 109 us
  Pallas kernels  53.7 us (49%)
  starting transfers between devices  42.1 us (39%)
  waiting for transfers between devices  8.7 us (8%)
  other arithmetic  2.02 us (2%)
  between operations  1.94 us (2%)
    ppermute x5, starting transfers between devices, exchange(): lax.ppermute(to_below, AXES, [(b, a) for a, b in up])  39.5 us
    pallas_call x1, Pallas kernels, program(): call(functools.partial(first_kernel, count), (shape(count, MX), shape(cou...  15.6 us
    pallas_call x1, Pallas kernels, program(): call(table_kernel, (shape(4, K, K, dtype=BF16), shape(K, K, dtype=BF16),...  15.4 us
    pallas_call x1, Pallas kernels, program(): call(functools.partial(second_kernel, count), (shape(K, MX), part, part,...  15.4 us
    ppermute x5, waiting for transfers between devices, exchange(): lax.ppermute(to_above, AXES, up)  8.58 us
    pallas_call x1, Pallas kernels, program(): call(functools.partial(pack_kernel, count), (shape(count + EXTRA, MX), sh...  3.48 us
    pallas_call x1, Pallas kernels, program(): call(restore_kernel, shape(K, MX), inputs=2, flops=2 * K * K * 3 * MX, da...  2.82 us
    ppermute x5, starting transfers between devices, exchange(): lax.ppermute(to_above, AXES, up)  2.69 us
  transfers between devices with their start and end apart: 10, of which 3 were waited for; matrix products, arithmetic and copies ran while one was open for 0% of the time, Pallas kernels for 17%

profile of v1, /device:TPU:1, one launch (start us, length us, event | category | flops | bytes accessed | tf_op | source)
XLA Modules:
  0.0 109.1 jit_solution(4537073585967946839)
XLA Ops:
  0.6 0.7 convert_element_type.7
  1.3 1.3 %slice_reduce_fusion = s32[]{:T(128)} fusion(s32[2,1024]{1,0:T(2,128)} %param.21), kind=kLoop, calls=%fused_computation | loop fusion | flops 1023 | bytes 4100 | tf_op jit(solution)/shard_map/reduce_sum | solution.py:458
  4.0 105.1 %conditional.1 = (f32[1024,256]{1,0:T(8,128)}, f32[2,64,128]{2,1,0:T(8,128)}) conditional(s32[]{:T(128)} %convert_element_type.6, (s32[2,1024]{1,0:T(2,128)}, f32[1024,256]{1,0:T(8,128)}, f32[2,64,128]{2,1,0:T(8,128)}, f32[64]{0:T(128)}, s32[4,128]{1,0:T(4,128)}, /*index=5*/f32[4,128]{1,0:T(4,128)}, s32[]{:T(128)}, f32[2,1024]{1,0:T(2,128)}, ...), branch_computations={%region_1.0_spmd, %region_2.0_spmd} | conditional | flops 18255708160 | bytes 63378356 | solution.py:460
  4.2 0.0 copy-start.16
  4.2 0.0 copy-start.17
  4.3 3.5 %pack.3 = (f32[616,256]{1,0:T(8,128)S(1)}, f32[616,256]{1,0:T(8,128)S(1)}, f32[8,128]{1,0:T(8,128)S(1)}, f32[8,128]{1,0:T(8,128)S(1)}) custom-call(s32[2,1024]{1,0:T(2,128)} %get-tuple-element.107.sign, f32[1024,256]{1,0:T(8,128)} %get-tuple-element.177.spectrum, f32[2,64,128]{2,1,0:T(8,128)} %get-tuple-element.179.currents, f32[1,64]{1,0:T(1,128)} %bitcast.22, ...), custom_call_target="tpu_custom_call" | custom-call | flops 1610612736 | bytes 1048576 | tf_op jit(solution)/shard_map/cond/branch_1_fun/pack/pallas_call | solution.py:387
  7.8 2.5 %collective-permute-start.10 = (f32[616,256]{1,0:T(8,128)S(1)}, f32[616,256]{1,0:T(8,128)S(1)}, u32[]{:S(2)}, u32[]{:S(2)}) collective-permute-start(f32[616,256]{1,0:T(8,128)S(1)} %get-tuple-element.113.own_up), channel_id=1, source_target_pairs={{0,1},{1,2},{2,3},{3,4},{4,5},{5,6},{6,7},{7,8},{8,9},{9,10},{10,1... | collective-permute-start | bytes 1892360 | tf_op jit(solution)/shard_map/cond/branch_1_fun/ppermute | solution.py:376
  10.3 9.2 %collective-permute-start.11 = (f32[616,256]{1,0:T(8,128)S(1)}, f32[616,256]{1,0:T(8,128)S(1)}, u32[]{:S(2)}, u32[]{:S(2)}) collective-permute-start(f32[616,256]{1,0:T(8,128)S(1)} %get-tuple-element.114.own_down), channel_id=1, source_target_pairs={{1,0},{2,1},{3,2},{4,3},{5,4},{6,5},{7,6},{8,7},{9,8},{10,9},{11,1... | collective-permute-start | bytes 1892360 | tf_op jit(solution)/shard_map/cond/branch_1_fun/ppermute | solution.py:377
  19.6 15.4 %tables.3 = (bf16[4,1024,1024]{2,1,0:T(8,128)(2,1)}, bf16[1024,1024]{1,0:T(8,128)(2,1)S(1)}, bf16[128,1024]{1,0:T(8,128)(2,1)S(1)}, f32[7,1024,128]{2,1,0:T(8,128)S(1)}, f32[384,256]{1,0:T(8,128)S(1)}) custom-call(s32[1]{0:T(128)} %bitcast.5.row, f32[8,128]{1,0:T(8,128)S(1)} %get-tuple-element.116.pos, s32[2,1024]{1,0:T(2,128)S(1)} %copy-done.13, ...), custom_call_target="tpu_custom_call" | custom-call | flops 8589934592 | bytes 12582912 | tf_op jit(solution)/shard_map/cond/branch_1_fun/tables/pallas_call | solution.py:394
  35.1 15.6 %first.3 = (f32[576,256]{1,0:T(8,128)S(1)}, f32[576,256]{1,0:T(8,128)S(1)}, f32[128,128]{1,0:T(8,128)S(1)}, f32[128,128]{1,0:T(8,128)S(1)}, f32[128,128]{1,0:T(8,128)S(1)}, /*index=5*/f32[256,384]{1,0:T(8,128)S(1)}) custom-call(s32[1]{0:T(128)} %bitcast.5.row, f32[616,256]{1,0:T(8,128)S(1)} %get-tuple-element.113.own_up, ...), custom_call_target="tpu_custom_call" | custom-call | flops 3221225472 | bytes 12582912 | tf_op jit(solution)/shard_map/cond/branch_1_fun/first/pallas_call | solution.py:404
  50.7 0.1 collective-permute-start.12
  50.8 7.2 %collective-permute-start.13 = (f32[576,256]{1,0:T(8,128)S(1)}, f32[576,256]{1,0:T(8,128)S(1)}, u32[]{:S(2)}, u32[]{:S(2)}) collective-permute-start(f32[576,256]{1,0:T(8,128)S(1)} %get-tuple-element.130.own_down), channel_id=1, source_target_pairs={{1,0},{2,1},{3,2},{4,3},{5,4},{6,5},{7,6},{8,7},{9,8},{10,9},{11,1... | collective-permute-start | bytes 1769480 | tf_op jit(solution)/shard_map/cond/branch_1_fun/ppermute | solution.py:377
  58.0 7.2 %collective-permute-start.15 = (f32[128,128]{1,0:T(8,128)S(1)}, f32[128,128]{1,0:T(8,128)S(1)}, u32[]{:S(2)}, u32[]{:S(2)}) collective-permute-start(f32[128,128]{1,0:T(8,128)S(1)} %get-tuple-element.133), channel_id=1, source_target_pairs={{1,0},{2,1},{3,2},{4,3},{5,4},{6,5},{7,6},{8,7},{9,8},{10,9},{11,1... | collective-permute-start | bytes 196616 | tf_op jit(solution)/shard_map/cond/branch_1_fun/ppermute | solution.py:377
  65.2 7.3 %collective-permute-done.14.part_below = f32[128,128]{1,0:T(8,128)S(1)} collective-permute-done((f32[128,128]{1,0:T(8,128)S(1)}, f32[128,128]{1,0:T(8,128)S(1)}, u32[]{:S(2)}, u32[]{:S(2)}) %collective-permute-start.14) | collective-permute-done | bytes 65568 | tf_op jit(solution)/shard_map/cond/branch_1_fun/ppermute | solution.py:376
  72.4 0.1 collective-permute-done.15.part_above
  72.5 0.1 broadcast_in_dim.8.mixing
  72.6 0.2 ocean.3
  72.9 8.2 %collective-permute-start.17 = (f32[72,128]{1,0:T(8,128)S(1)}, f32[72,128]{1,0:T(8,128)S(1)}, u32[]{:S(2)}, u32[]{:S(2)}) collective-permute-start(f32[72,128]{1,0:T(8,128)S(1)} %get-tuple-element.136.ocean_own), channel_id=1, source_target_pairs={{1,0},{2,1},{3,2},{4,3},{5,4},{6,5},{7,6},{8,7},{9,8},{10,9},{11,1... | collective-permute-start | bytes 110600 | tf_op jit(solution)/shard_map/cond/branch_1_fun/ppermute | solution.py:377
  81.1 1.3 %collective-permute-done.16.ocean_below = f32[72,128]{1,0:T(8,128)S(1)} collective-permute-done((f32[72,128]{1,0:T(8,128)S(1)}, f32[72,128]{1,0:T(8,128)S(1)}, u32[]{:S(2)}, u32[]{:S(2)}) %collective-permute-start.16) | collective-permute-done | bytes 36896 | tf_op jit(solution)/shard_map/cond/branch_1_fun/ppermute | solution.py:376
  82.4 15.4 %second.3 = (f32[1024,256]{1,0:T(8,128)S(1)}, f32[128,128]{1,0:T(8,128)S(1)}, f32[128,128]{1,0:T(8,128)S(1)}, f32[128,128]{1,0:T(8,128)S(1)}) custom-call(f32[576,256]{1,0:T(8,128)S(1)} %get-tuple-element.129.own_up, f32[576,256]{1,0:T(8,128)S(1)} %get-tuple-element.130.own_down, f32[576,256]{1,0:T(8,128)S(1)} %collective-permute-done.12.from_below, ...), custom_call_target="tpu_custom_call" | custom-call | flops 3221225472 | bytes 12582912 | tf_op jit(solution)/shard_map/cond/branch_1_fun/second/pallas_call | solution.py:418
  97.8 0.1 collective-permute-start.18
  97.9 7.6 %collective-permute-start.19 = (f32[128,128]{1,0:T(8,128)S(1)}, f32[128,128]{1,0:T(8,128)S(1)}, u32[]{:S(2)}, u32[]{:S(2)}) collective-permute-start(f32[128,128]{1,0:T(8,128)S(1)} %get-tuple-element.143), channel_id=1, source_target_pairs={{1,0},{2,1},{3,2},{4,3},{5,4},{6,5},{7,6},{8,7},{9,8},{10,9},{11,1... | collective-permute-start | bytes 196616 | tf_op jit(solution)/shard_map/cond/branch_1_fun/ppermute | solution.py:377
  105.5 2.8 %restore.3 = f32[1024,256]{1,0:T(8,128)} custom-call(f32[1024,256]{1,0:T(8,128)S(1)} %get-tuple-element.138.spectra, bf16[1024,1024]{1,0:T(8,128)(2,1)S(1)} %get-tuple-element.139.back), custom_call_target="tpu_custom_call" | custom-call | flops 1610612736 | bytes 4194304 | tf_op jit(solution)/shard_map/cond/branch_1_fun/restore/pallas_call | solution.py:425
  108.4 0.7 ocean_end.3
  (35 shorter events, 0.1 us)
Async XLA Ops:
  4.2 15.3 %copy-start.13 = (s32[2,1024]{1,0:T(2,128)S(1)}, s32[2,1024]{1,0:T(2,128)}, u32[]{:S(2)}) copy-start(s32[2,1024]{1,0:T(2,128)} %get-tuple-element.107.sign) | copy-start | bytes 24580 | tf_op jit(solution)/shard_map/cond
  4.2 15.3 %copy-start.15 = (bf16[128,1024]{1,0:T(8,128)(2,1)S(1)}, bf16[128,1024]{1,0:T(8,128)(2,1)}, u32[]{:S(2)}) copy-start(bf16[128,1024]{1,0:T(8,128)(2,1)} %get-tuple-element.195.stokes_table) | copy-start | bytes 786436 | tf_op jit(solution)/shard_map/cond
  4.2 15.3 %copy-start.16 = (s32[4,2,1024]{2,1,0:T(2,128)S(1)}, s32[4,2,1024]{2,1,0:T(2,128)}, u32[]{:S(2)}) copy-start(s32[4,2,1024]{2,1,0:T(2,128)} %get-tuple-element.119.quad_index) | copy-start | bytes 98308 | tf_op jit(solution)/shard_map/cond
  4.2 15.3 %copy-start.17 = (f32[4,2,1024]{2,1,0:T(2,128)S(1)}, f32[4,2,1024]{2,1,0:T(2,128)}, u32[]{:S(2)}) copy-start(f32[4,2,1024]{2,1,0:T(2,128)} %get-tuple-element.120.quad_weight) | copy-start | bytes 98308 | tf_op jit(solution)/shard_map/cond
  4.2 15.3 %copy-start.18 = (f32[2,1024]{1,0:T(2,128)S(1)}, f32[2,1024]{1,0:T(2,128)}, u32[]{:S(2)}) copy-start(f32[2,1024]{1,0:T(2,128)} %get-tuple-element.191.courant) | copy-start | bytes 24580 | tf_op jit(solution)/shard_map/cond
  4.3 15.3 %copy-start.20 = (f32[1024]{0:T(1024)S(1)}, f32[1024]{0:T(1024)}, u32[]{:S(2)}) copy-start(f32[1024]{0:T(1024)} %get-tuple-element.211) | copy-start | bytes 12292 | tf_op jit(solution)/shard_map/cond
  4.3 15.3 %copy-start.21 = (s32[4,256]{1,0:T(4,128)S(1)}, s32[4,256]{1,0:T(4,128)}, u32[]{:S(2)}) copy-start(s32[4,256]{1,0:T(4,128)} %get-tuple-element.197.point_index) | copy-start | bytes 12292 | tf_op jit(solution)/shard_map/cond
  4.3 15.3 %copy-start.22 = (f32[4,256]{1,0:T(4,128)S(1)}, f32[4,256]{1,0:T(4,128)}, u32[]{:S(2)}) copy-start(f32[4,256]{1,0:T(4,128)} %get-tuple-element.199.point_weight) | copy-start | bytes 12292 | tf_op jit(solution)/shard_map/cond
  7.8 27.3 %collective-permute-start.10 = (f32[616,256]{1,0:T(8,128)S(1)}, f32[616,256]{1,0:T(8,128)S(1)}, u32[]{:S(2)}, u32[]{:S(2)}) collective-permute-start(f32[616,256]{1,0:T(8,128)S(1)} %get-tuple-element.113.own_up), channel_id=1, source_target_pairs={{0,1},{1,2},{2,3},{3,4},{4,5},{5,6},{6,7},{7,8},{8,9},{9,10},{10,1... | collective-permute-start | bytes 1892360 | tf_op jit(solution)/shard_map/cond/branch_1_fun/ppermute | solution.py:376
  10.3 24.8 %collective-permute-start.11 = (f32[616,256]{1,0:T(8,128)S(1)}, f32[616,256]{1,0:T(8,128)S(1)}, u32[]{:S(2)}, u32[]{:S(2)}) collective-permute-start(f32[616,256]{1,0:T(8,128)S(1)} %get-tuple-element.114.own_down), channel_id=1, source_target_pairs={{1,0},{2,1},{3,2},{4,3},{5,4},{6,5},{7,6},{8,7},{9,8},{10,9},{11,1... | collective-permute-start | bytes 1892360 | tf_op jit(solution)/shard_map/cond/branch_1_fun/ppermute | solution.py:377
  19.6 15.5 %copy-start.3 = (s32[4,128]{1,0:T(4,128)S(1)}, s32[4,128]{1,0:T(4,128)}, u32[]{:S(2)}) copy-start(s32[4,128]{1,0:T(4,128)} %get-tuple-element.183.ocean_index) | copy-start | bytes 6148 | tf_op jit(solution)/shard_map/cond
  19.6 15.5 %copy-start.5 = (f32[4,128]{1,0:T(4,128)S(1)}, f32[4,128]{1,0:T(4,128)}, u32[]{:S(2)}) copy-start(f32[4,128]{1,0:T(4,128)} %get-tuple-element.185.ocean_weight) | copy-start | bytes 6148 | tf_op jit(solution)/shard_map/cond
  35.1 37.5 %copy-start.11 = (f32[64]{0:T(128)S(1)}, f32[64]{0:T(128)}, u32[]{:S(2)}) copy-start(f32[64]{0:T(128)} %get-tuple-element.215) | copy-start | bytes 772 | tf_op jit(solution)/shard_map/cond
  35.1 37.5 %copy-start.1 = (f32[2,64,128]{2,1,0:T(8,128)S(1)}, f32[2,64,128]{2,1,0:T(8,128)}, u32[]{:S(2)}) copy-start(f32[2,64,128]{2,1,0:T(8,128)} %get-tuple-element.179.currents) | copy-start | bytes 196612 | tf_op jit(solution)/shard_map/cond
  35.1 37.5 %copy-start.7 = (f32[128]{0:T(128)S(1)}, f32[128]{0:T(128)}, u32[]{:S(2)}) copy-start(f32[128]{0:T(128)} %get-tuple-element.213) | copy-start | bytes 1540 | tf_op jit(solution)/shard_map/cond
  35.1 37.5 %copy-start.9 = (f32[64]{0:T(128)S(1)}, f32[64]{0:T(128)}, u32[]{:S(2)}) copy-start(f32[64]{0:T(128)} %get-tuple-element.205) | copy-start | bytes 772 | tf_op jit(solution)/shard_map/cond
  50.7 31.7 %collective-permute-start.12 = (f32[576,256]{1,0:T(8,128)S(1)}, f32[576,256]{1,0:T(8,128)S(1)}, u32[]{:S(2)}, u32[]{:S(2)}) collective-permute-start(f32[576,256]{1,0:T(8,128)S(1)} %get-tuple-element.129.own_up), channel_id=1, source_target_pairs={{0,1},{1,2},{2,3},{3,4},{4,5},{5,6},{6,7},{7,8},{8,9},{9,10},{10,1... | collective-permute-start | bytes 1769480 | tf_op jit(solution)/shard_map/cond/branch_1_fun/ppermute | solution.py:376
  50.8 31.6 %collective-permute-start.13 = (f32[576,256]{1,0:T(8,128)S(1)}, f32[576,256]{1,0:T(8,128)S(1)}, u32[]{:S(2)}, u32[]{:S(2)}) collective-permute-start(f32[576,256]{1,0:T(8,128)S(1)} %get-tuple-element.130.own_down), channel_id=1, source_target_pairs={{1,0},{2,1},{3,2},{4,3},{5,4},{6,5},{7,6},{8,7},{9,8},{10,9},{11,1... | collective-permute-start | bytes 1769480 | tf_op jit(solution)/shard_map/cond/branch_1_fun/ppermute | solution.py:377
  58.0 14.4 %collective-permute-start.14 = (f32[128,128]{1,0:T(8,128)S(1)}, f32[128,128]{1,0:T(8,128)S(1)}, u32[]{:S(2)}, u32[]{:S(2)}) collective-permute-start(f32[128,128]{1,0:T(8,128)S(1)} %get-tuple-element.131), channel_id=1, source_target_pairs={{0,1},{1,2},{2,3},{3,4},{4,5},{5,6},{6,7},{7,8},{8,9},{9,10},{10,1... | collective-permute-start | bytes 196616 | tf_op jit(solution)/shard_map/cond/branch_1_fun/ppermute | solution.py:376
  58.0 14.5 %collective-permute-start.15 = (f32[128,128]{1,0:T(8,128)S(1)}, f32[128,128]{1,0:T(8,128)S(1)}, u32[]{:S(2)}, u32[]{:S(2)}) collective-permute-start(f32[128,128]{1,0:T(8,128)S(1)} %get-tuple-element.133), channel_id=1, source_target_pairs={{1,0},{2,1},{3,2},{4,3},{5,4},{6,5},{7,6},{8,7},{9,8},{10,9},{11,1... | collective-permute-start | bytes 196616 | tf_op jit(solution)/shard_map/cond/branch_1_fun/ppermute | solution.py:377
  72.9 9.6 %collective-permute-start.16 = (f32[72,128]{1,0:T(8,128)S(1)}, f32[72,128]{1,0:T(8,128)S(1)}, u32[]{:S(2)}, u32[]{:S(2)}) collective-permute-start(f32[72,128]{1,0:T(8,128)S(1)} %get-tuple-element.136.ocean_own), channel_id=1, source_target_pairs={{0,1},{1,2},{2,3},{3,4},{4,5},{5,6},{6,7},{7,8},{8,9},{9,10},{10,1... | collective-permute-start | bytes 110600 | tf_op jit(solution)/shard_map/cond/branch_1_fun/ppermute | solution.py:376
  72.9 9.6 %collective-permute-start.17 = (f32[72,128]{1,0:T(8,128)S(1)}, f32[72,128]{1,0:T(8,128)S(1)}, u32[]{:S(2)}, u32[]{:S(2)}) collective-permute-start(f32[72,128]{1,0:T(8,128)S(1)} %get-tuple-element.136.ocean_own), channel_id=1, source_target_pairs={{1,0},{2,1},{3,2},{4,3},{5,4},{6,5},{7,6},{8,7},{9,8},{10,9},{11,1... | collective-permute-start | bytes 110600 | tf_op jit(solution)/shard_map/cond/branch_1_fun/ppermute | solution.py:377
  97.8 10.6 %collective-permute-start.18 = (f32[128,128]{1,0:T(8,128)S(1)}, f32[128,128]{1,0:T(8,128)S(1)}, u32[]{:S(2)}, u32[]{:S(2)}) collective-permute-start(f32[128,128]{1,0:T(8,128)S(1)} %get-tuple-element.141), channel_id=1, source_target_pairs={{0,1},{1,2},{2,3},{3,4},{4,5},{5,6},{6,7},{7,8},{8,9},{9,10},{10,1... | collective-permute-start | bytes 196616 | tf_op jit(solution)/shard_map/cond/branch_1_fun/ppermute | solution.py:376
  97.9 10.5 %collective-permute-start.19 = (f32[128,128]{1,0:T(8,128)S(1)}, f32[128,128]{1,0:T(8,128)S(1)}, u32[]{:S(2)}, u32[]{:S(2)}) collective-permute-start(f32[128,128]{1,0:T(8,128)S(1)} %get-tuple-element.143), channel_id=1, source_target_pairs={{1,0},{2,1},{3,2},{4,3},{5,4},{6,5},{7,6},{8,7},{9,8},{10,9},{11,1... | collective-permute-start | bytes 196616 | tf_op jit(solution)/shard_map/cond/branch_1_fun/ppermute | solution.py:377
